TPU v7x, 512 devices: a whole 4x4x16 slice. The times are simulated.
512 devices in a mesh: query: 32 (over z, core), passage: 16 (over x, y).
Axes of the slice: x: 4, y: 4, z: 16, core: 2. Of those that a mesh axis runs over, the one named last changes fastest.
Arguments:
- queries: bfloat16 [2048, 32, 128], P(('query', 'passage')), may hold values from -60 to 60
- hidden: bfloat16 [2048, 180, 768], P(('query', 'passage')), may hold values from -24 to 24
- proj: bfloat16 [768, 128], replicated, may hold values from -0.21875 to 0.21875
- lists: int32 [2048, 64], P(('query', 'passage')), may hold values from 0 to 63
Outputs:
- losses: float32 [2048], P(('query', 'passage'))
- w_grad: float32 [768, 128], P('passage')
Inputs may be any that keep to these rules, and one draw needn't show every extreme that they name: `lists`: queries of one row only list passages of that same row; entry 0 of each list is the query's positive passage.
All inputs are finite; a program needn't handle non-finite values.
Results may differ from a plain program's by a relative error of at most 0.0075.
The roundings to bfloat16 on the way count: a program that leaves them out, or rounds other values in their place, can miss the bound.
Values may be sent and summed in bfloat16 or wider, within the bound.
A program may use at most 64 MiB of HBM per device.

v0:
```python
import jax
import jax.numpy as jnp
from jax import lax
from jax.sharding import PartitionSpec as P

BETA = 4.0
EPS = 1e-06


def body(queries, hidden, proj, lists):
    qcount, qtok, width = queries.shape
    pcount, ptok, hwidth = hidden.shape
    nside = lax.axis_size("passage")
    prow = pcount * nside
    total = qcount * lax.axis_size("query") * nside
    hidden_flat = hidden.reshape(-1, hwidth)
    flat = jnp.dot(hidden_flat, proj, preferred_element_type=jnp.float32)
    norm = jnp.sqrt(jnp.sum(flat * flat, axis=1, keepdims=True) + EPS)
    unit = flat / norm
    embed = unit.astype(jnp.bfloat16).reshape(pcount, ptok, width)
    gathered = lax.all_gather(queries, "passage", axis=0, tiled=True)
    qflat = gathered.reshape(-1, width)

    def score_single(emb):
        sims = lax.dot_general(
            emb, qflat, (((1,), (1,)), ((), ())), preferred_element_type=jnp.float32
        )
        lse = jax.nn.logsumexp(BETA * sims, axis=0)
        return jnp.sum(lse.reshape(-1, qtok), axis=1) / BETA

    scores = lax.map(score_single, embed).T
    mine = lax.all_to_all(scores, "passage", split_axis=0, concat_axis=1, tiled=True)
    columns = jnp.arange(prow, dtype=jnp.int32)
    onehot = (lists[:, :, None] == columns[None, None, :]).astype(jnp.float32)
    listed = jnp.einsum("qkp,qp->qk", onehot, mine, precision=lax.Precision.HIGHEST)
    losses = jax.nn.logsumexp(listed, axis=1) - listed[:, 0]
    probs = jax.nn.softmax(listed, axis=1)
    target = (jnp.arange(listed.shape[1], dtype=jnp.int32) == 0).astype(jnp.float32)
    coef = (
        jnp.einsum("qkp,qk->qp", onehot, probs - target[None, :], precision=lax.Precision.HIGHEST)
        / total
    )
    coef_home = lax.all_to_all(coef, "passage", split_axis=1, concat_axis=0, tiled=True)
    grad_qflat = gathered.reshape(-1, width)

    def grad_single(args):
        emb, column = args
        sims = lax.dot_general(
            emb, grad_qflat, (((1,), (1,)), ((), ())), preferred_element_type=jnp.float32
        )
        probs = jax.nn.softmax(BETA * sims, axis=0)
        weight = (probs * jnp.repeat(column, qtok)[None, :]).astype(jnp.bfloat16)
        return jnp.dot(weight, grad_qflat, preferred_element_type=jnp.float32)

    d_embed = lax.map(grad_single, (embed, coef_home.T))
    d_rows = d_embed.reshape(-1, width)
    d_flat = ((d_rows - unit * jnp.sum(d_rows * unit, axis=1, keepdims=True)) / norm).astype(
        jnp.bfloat16
    )
    partial_grad = lax.dot_general(
        hidden_flat, d_flat, (((0,), (0,)), ((), ())), preferred_element_type=jnp.float32
    )
    share = hwidth // nside
    full_grad = lax.psum(partial_grad, ("query", "passage"))
    w_grad = lax.dynamic_slice_in_dim(full_grad, lax.axis_index("passage") * share, share, 0)
    return (losses, w_grad)


def solution(mesh):
    placed = (
        P(("query", "passage"), None, None),
        P(("query", "passage"), None, None),
        P(),
        P(("query", "passage"), None),
    )
    return jax.shard_map(
        body,
        mesh=mesh,
        in_specs=placed,
        out_specs=(P(("query", "passage")), P("passage", None)),
        check_vma=False,
    )
```

profile of v0, /device:TPU:2, one launch (start us, length us, event | category | flops | bytes accessed | tf_op | source)
XLA Modules:
  0.0 561.4 jit_solution(6270691283780664740)
XLA Ops:
  7.2 1.4 copy.11
  10.2 26.8 %all_gather.3 = bf16[64,32,128]{2,1,0:T(8,128)(2,1)S(1)} all-gather(bf16[4,32,128]{2,1,0:T(8,128)(2,1)S(1)} %copy-done.6), channel_id=1, replica_groups=mesh['query'=32,'passage'=16] {'passage'}, dimensions={0}, use_global_device_ids=true | all-gather | bytes 557056 | tf_op jit(solution)/shard_map/all_gather | solution.py:21
  37.0 4.4 while.20
  42.1 5.4 all-to-all-start
  47.6 6.2 %all-to-all-done = f32[16,4,4]{1,2,0:T(4,128)S(1)} async-done(((f32[16,4,4]{1,2,0:T(4,128)}), f32[16,4,4]{1,2,0:T(4,128)S(1)}, u32[]{:S(2)}, u32[]{:S(2)}) %all-to-all-start) | async-done | bytes 1056 | tf_op jit(solution)/shard_map/all_to_all | solution.py:32
  55.5 0.6 copy.14
  56.1 4.8 all-to-all-start.1
  60.9 6.2 %all-to-all-done.1 = f32[4,16,4]{2,0,1:T(4,128)S(1)} async-done(((f32[4,16,4]{2,0,1:T(4,128)}), f32[4,16,4]{2,0,1:T(4,128)S(1)}, u32[]{:S(2)}, u32[]{:S(2)}) %all-to-all-start.1) | async-done | bytes 1056 | tf_op jit(solution)/shard_map/all_to_all | solution.py:43
  67.2 16.0 %while.21 = (s32[]{:T(128)}, f32[4,180,128]{2,1,0:T(8,128)}, bf16[4,180,128]{2,1,0:T(8,128)(2,1)S(1)}, bf16[2048,128]{1,0:T(8,128)(2,1)S(1)}, f32[4,64]{1,0:T(4,128)S(1)}, /*index=5*/s32[]{:T(128)}) while((s32[]{:T(128)}, f32[4,180,128]{2,1,0:T(8,128)}, bf16[4,180,128]{2,1,0:T(8,128)(2,1)S(1)}, bf16[2048,128]{1,0:T(8,128)(2,1)S(1)}, ...), condition=%wide.region_12.13_spmd, body=%wide.region_9.0_spmd.sunk | while | flops 191688704 | bytes 5761993 | solution.py:55
  67.2 1.1 fusion.44
  68.4 0.7 mul.57
  69.1 1.0 fusion.46
  70.1 1.1 fusion.47
  71.2 1.1 fusion.44
  72.4 0.7 mul.57
  73.1 1.0 fusion.46
  74.1 1.1 fusion.47
  75.2 1.1 fusion.44
  76.4 0.7 mul.57
  77.1 1.0 fusion.46
  78.1 1.1 fusion.47
  79.3 1.1 fusion.44
  80.5 0.7 mul.57
  81.1 1.0 fusion.46
  82.2 1.1 fusion.47
  83.3 1.0 reshape.67
  84.3 1.3 multiply_reduce_fusion
  85.6 2.3 convolution_bitcast_fusion.1
  88.0 1.2 fusion.18
  89.2 463.7 %all-reduce.2.cloned.1.call-done = f32[768,128]{0,1:T(8,128)} async-done(((f32[768,128]{0,1:T(8,128)}), f32[768,128]{0,1:T(8,128)}) %all-reduce.2.cloned.1.call-update) | async-done | bytes 393232 | tf_op jit(solution)/shard_map/psum | solution.py:64
  552.8 1.0 constant_dynamic-slice_fusion.1
  553.8 0.7 copy.16
  (118 shorter events, 8.6 us)
Async XLA Ops:
  7.2 1.7 copy-start
  8.9 1.3 copy-start.6
  9.4 0.7 copy-start.1
  9.5 0.7 copy-start.5
  37.0 16.8 %copy-start.12 = (s32[4,64]{1,0:T(4,128)S(1)}, s32[4,64]{1,0:T(4,128)}, u32[]{:S(2)}) copy-start(s32[4,64]{1,0:T(4,128)} %param.11) | copy-start | bytes 3076
  42.1 11.6 %all-to-all-start = ((f32[16,4,4]{1,2,0:T(4,128)}), f32[16,4,4]{1,2,0:T(4,128)S(1)}, u32[]{:S(2)}, u32[]{:S(2)}) async-start(f32[16,4,4]{1,2,0:T(4,128)} %copy.12), calls=%async_computation | async-start | bytes 65536 | tf_op jit(solution)/shard_map/all_to_all | solution.py:32
  54.2 13.0 %copy-start.3 = (f32[4,1,64]{0,2,1:T(8,128)}, f32[4,1,64]{0,2,1:T(8,128)S(1)}, u32[]{:S(2)}) copy-start(f32[4,1,64]{0,2,1:T(8,128)S(1)} %copy.18) | copy-start | bytes 3076
  54.3 0.6 copy-start.7
  56.1 11.1 %all-to-all-start.1 = ((f32[4,16,4]{2,0,1:T(4,128)}), f32[4,16,4]{2,0,1:T(4,128)S(1)}, u32[]{:S(2)}, u32[]{:S(2)}) async-start(f32[4,16,4]{2,0,1:T(4,128)} %copy.14), calls=%async_computation.1 | async-start | bytes 65536 | tf_op jit(solution)/shard_map/all_to_all | solution.py:43
  60.8 492.0 %all-reduce.2.cloned.1.call-start = ((), (), s32[]{:S(2)}) async-start(), calls=%async_computation.2 | async-start | bytes 786432 | tf_op jit(solution)/shard_map/psum | solution.py:64
  67.2 1.1 copy-start.10
  69.1 1.0 copy-start.2
  69.1 1.0 copy-start.4
  70.1 1.1 copy-start.11
  71.2 1.1 copy-start.10
  73.1 1.0 copy-start.2
  73.1 1.0 copy-start.4
  74.1 1.1 copy-start.11
  75.2 1.1 copy-start.10
  77.1 1.0 copy-start.2
  77.1 1.0 copy-start.4
  78.1 1.1 copy-start.11
  79.3 1.1 copy-start.10
  81.1 1.0 copy-start.2
  81.1 1.0 copy-start.4
  82.1 1.1 copy-start.11
  85.6 2.4 copy-start.8
  85.6 2.4 copy-start.9
Sparse Core Ops, SparseCore 0:
  88.1 464.7 all-reduce.1
where the time goes:
time: 562 us; the launch traced here: 561 us
  waiting for transfers between devices  476 us (85%)
  blocking collectives  26.8 us (5%)
  matrix products  14.4 us (3%)
  between operations  14.2 us (3%)
  local copies, waits for them, and re-layouts  10.5 us (2%)
  starting transfers between devices  10.2 us (2%)
  other arithmetic  8.8 us (2%)
    psum x1, waiting for transfers between devices, body(): full_grad = lax.psum(partial_grad, ('query', 'passage'))  464 us
    all_gather x1, blocking collectives, body(): gathered = lax.all_gather(queries, 'passage', axis=0, tiled=True)  26.8 us
  transfers between devices with their start and end apart: 3, of which 3 were waited for; matrix products, arithmetic and copies ran while one was open for 0% of the time, Pallas kernels for 0%

commit v1 on v0

--- a/solution.py
+++ b/solution.py
@@ -61,7 +61,7 @@
         hidden_flat, d_flat, (((0,), (0,)), ((), ())), preferred_element_type=jnp.float32
     )
     share = hwidth // nside
-    full_grad = lax.psum(partial_grad, ("query", "passage"))
+    full_grad = lax.psum(lax.psum(partial_grad, "query"), "passage")
     w_grad = lax.dynamic_slice_in_dim(full_grad, lax.axis_index("passage") * share, share, 0)
     return (losses, w_grad)
 

time: 562 us -> 414 us (0.74)
  the two profiles are of different devices: /device:TPU:2 before, /device:TPU:32 now
where the time goes in v1:
time: 414 us; the launch traced here: 413 us
  waiting for transfers between devices  333 us (80%)
  blocking collectives  24.3 us (6%)
  matrix products  14.3 us (3%)
  between operations  14.2 us (3%)
  local copies, waits for them, and re-layouts  10.5 us (3%)
  other arithmetic  8.73 us (2%)
  starting transfers between devices  8.49 us (2%)
    psum x2, waiting for transfers between devices, body(): full_grad = lax.psum(lax.psum(partial_grad, 'query'), 'passage')  317 us
    all_gather x1, blocking collectives, body(): gathered = lax.all_gather(queries, 'passage', axis=0, tiled=True)  24.3 us
  transfers between devices with their start and end apart: 4, of which 4 were waited for; matrix products, arithmetic and copies ran while one was open for 0% of the time, Pallas kernels for 0%

profile of v1, /device:TPU:32, one launch (start us, length us, event | category | flops | bytes accessed | tf_op | source)
XLA Modules:
  0.0 413.5 jit_solution(6533797748274947541)
XLA Ops:
  7.2 1.4 copy.11
  10.2 24.3 %all_gather.3 = bf16[64,32,128]{2,1,0:T(8,128)(2,1)S(1)} all-gather(bf16[4,32,128]{2,1,0:T(8,128)(2,1)S(1)} %copy-done.6), channel_id=1, replica_groups=mesh['query'=32,'passage'=16] {'passage'}, dimensions={0}, use_global_device_ids=true | all-gather | bytes 557056 | tf_op jit(solution)/shard_map/all_gather | solution.py:21
  34.5 4.4 %while.20 = (s32[]{:T(128)}, f32[4,64]{1,0:T(4,128)S(1)}, bf16[4,180,128]{2,1,0:T(8,128)(2,1)S(1)}, bf16[2048,128]{1,0:T(8,128)(2,1)S(1)}, s32[]{:T(128)}, /*index=5*/s32[]{:T(128)}) while((s32[]{:T(128)}, f32[4,64]{1,0:T(4,128)S(1)}, bf16[4,180,128]{2,1,0:T(8,128)(2,1)S(1)}, bf16[2048,128]{1,0:T(8,128)(2,1)S(1)}, s32[]{:T(128)}, ...), condition=%wide.region_5.6_spmd, body=%wide.region_1.5_spmd.sunk | while | flops 95856640 | bytes 3628373 | solution.py:31
  39.6 4.9 %all-to-all-start = ((f32[16,4,4]{1,2,0:T(4,128)}), f32[16,4,4]{1,2,0:T(4,128)S(1)}, u32[]{:S(2)}, u32[]{:S(2)}) async-start(f32[16,4,4]{1,2,0:T(4,128)} %copy.12), calls=%async_computation | async-start | bytes 65536 | tf_op jit(solution)/shard_map/all_to_all | solution.py:32
  44.5 7.6 %all-to-all-done = f32[16,4,4]{1,2,0:T(4,128)S(1)} async-done(((f32[16,4,4]{1,2,0:T(4,128)}), f32[16,4,4]{1,2,0:T(4,128)S(1)}, u32[]{:S(2)}, u32[]{:S(2)}) %all-to-all-start) | async-done | bytes 1056 | tf_op jit(solution)/shard_map/all_to_all | solution.py:32
  54.4 3.5 all-to-all-start.1
  57.9 7.5 %all-to-all-done.1 = f32[4,16,4]{2,0,1:T(4,128)S(1)} async-done(((f32[4,16,4]{2,0,1:T(4,128)}), f32[4,16,4]{2,0,1:T(4,128)S(1)}, u32[]{:S(2)}, u32[]{:S(2)}) %all-to-all-start.1) | async-done | bytes 1056 | tf_op jit(solution)/shard_map/all_to_all | solution.py:43
  65.5 16.0 %while.21 = (s32[]{:T(128)}, f32[4,180,128]{2,1,0:T(8,128)}, bf16[4,180,128]{2,1,0:T(8,128)(2,1)S(1)}, bf16[2048,128]{1,0:T(8,128)(2,1)S(1)}, f32[4,64]{1,0:T(4,128)S(1)}, /*index=5*/s32[]{:T(128)}) while((s32[]{:T(128)}, f32[4,180,128]{2,1,0:T(8,128)}, bf16[4,180,128]{2,1,0:T(8,128)(2,1)S(1)}, bf16[2048,128]{1,0:T(8,128)(2,1)S(1)}, ...), condition=%wide.region_12.13_spmd, body=%wide.region_9.0_spmd.sunk | while | flops 191688704 | bytes 5761993 | solution.py:55
  65.5 1.1 fusion.44
  66.7 0.7 mul.57
  67.4 1.0 fusion.46
  68.4 1.1 fusion.47
  69.5 1.1 fusion.44
  70.7 0.7 mul.57
  71.4 1.0 fusion.46
  72.4 1.1 fusion.47
  73.5 1.1 fusion.44
  74.7 0.7 mul.57
  75.4 1.0 fusion.46
  76.4 1.1 fusion.47
  77.5 1.1 fusion.44
  78.7 0.7 mul.57
  79.4 1.0 fusion.46
  80.4 1.1 fusion.47
  81.5 1.0 reshape.67
  82.5 1.3 multiply_reduce_fusion
  83.8 2.3 convolution_bitcast_fusion.1
  86.3 200.4 %all-reduce.3.cloned.1.call-done = f32[768,128]{0,1:T(8,128)} async-done(((f32[768,128]{0,1:T(8,128)}), f32[768,128]{0,1:T(8,128)}) %all-reduce.3.cloned.1.call-update) | async-done | bytes 393232 | tf_op jit(solution)/shard_map/psum | solution.py:64
  286.8 1.2 fusion.18
  288.0 117.0 %all-reduce.5.cloned.1.call-done = f32[768,128]{0,1:T(8,128)} async-done(((f32[768,128]{0,1:T(8,128)}), f32[768,128]{0,1:T(8,128)}) %all-reduce.5.cloned.1.call-update) | async-done | bytes 393232 | tf_op jit(solution)/shard_map/psum | solution.py:64
  405.0 1.0 constant_dynamic-slice_fusion.1
  405.9 0.7 copy.16
  (121 shorter events, 9.3 us)
Async XLA Ops:
  7.2 1.7 copy-start
  8.9 1.3 copy-start.6
  9.4 0.7 copy-start.1
  9.5 0.7 copy-start.5
  34.5 17.7 %copy-start.12 = (s32[4,64]{1,0:T(4,128)S(1)}, s32[4,64]{1,0:T(4,128)}, u32[]{:S(2)}) copy-start(s32[4,64]{1,0:T(4,128)} %param.11) | copy-start | bytes 3076
  39.6 12.6 %all-to-all-start = ((f32[16,4,4]{1,2,0:T(4,128)}), f32[16,4,4]{1,2,0:T(4,128)S(1)}, u32[]{:S(2)}, u32[]{:S(2)}) async-start(f32[16,4,4]{1,2,0:T(4,128)} %copy.12), calls=%async_computation | async-start | bytes 65536 | tf_op jit(solution)/shard_map/all_to_all | solution.py:32
  52.6 12.9 %copy-start.3 = (f32[4,1,64]{0,2,1:T(8,128)}, f32[4,1,64]{0,2,1:T(8,128)S(1)}, u32[]{:S(2)}) copy-start(f32[4,1,64]{0,2,1:T(8,128)S(1)} %copy.18) | copy-start | bytes 3076
  52.6 0.6 copy-start.7
  54.4 11.0 %all-to-all-start.1 = ((f32[4,16,4]{2,0,1:T(4,128)}), f32[4,16,4]{2,0,1:T(4,128)S(1)}, u32[]{:S(2)}, u32[]{:S(2)}) async-start(f32[4,16,4]{2,0,1:T(4,128)} %copy.14), calls=%async_computation.1 | async-start | bytes 65536 | tf_op jit(solution)/shard_map/all_to_all | solution.py:43
  57.9 228.8 %all-reduce.3.cloned.1.call-start = ((), (), s32[]{:S(2)}) async-start(), calls=%async_computation.2 | async-start | bytes 786432 | tf_op jit(solution)/shard_map/psum | solution.py:64
  65.5 1.1 copy-start.10
  67.4 1.0 copy-start.2
  67.4 1.0 copy-start.4
  68.4 1.1 copy-start.11
  69.5 1.1 copy-start.10
  71.4 1.0 copy-start.2
  71.4 1.0 copy-start.4
  72.4 1.1 copy-start.11
  73.5 1.1 copy-start.10
  75.4 1.0 copy-start.2
  75.4 1.0 copy-start.4
  76.4 1.1 copy-start.11
  77.5 1.1 copy-start.10
  79.4 1.0 copy-start.2
  79.4 1.0 copy-start.4
  80.4 1.1 copy-start.11
  83.8 202.9 %copy-start.8 = (f32[4]{0:T(128)S(1)}, f32[4]{0:T(128)}, u32[]{:S(2)}) copy-start(f32[4]{0:T(128)} %copy-done.7) | copy-start | bytes 52
  83.8 202.9 %copy-start.9 = (f32[4]{0:T(128)S(1)}, f32[4]{0:T(128)}, u32[]{:S(2)}) copy-start(f32[4]{0:T(128)} %get-tuple-element.60) | copy-start | bytes 52
  86.2 318.7 %all-reduce.5.cloned.1.call-start = ((), (), s32[]{:S(2)}) async-start(), calls=%async_computation.3 | async-start | bytes 786432 | tf_op jit(solution)/shard_map/psum | solution.py:64
Sparse Core Ops, SparseCore 0:
  86.3 200.3 all-reduce.2
  290.3 114.6 all-reduce.4
